TPU v7x, 256 devices: a whole 4x4x8 slice. The times are simulated.
256 devices in a mesh: tm: 32 (over y, x, core), tensor: 8 (over z).
Axes of the slice: x: 4, y: 4, z: 8, core: 2. Of those that a mesh axis runs over, the one named last changes fastest.
Arguments:
- tokens: bfloat16 [32, 768, 2048], P('tm', None, 'tensor'), may hold values from -12 to 12
- action_rows: bfloat16 [32, 2048], P('tm', 'tensor'), may hold values from -6 to 6
- pair_index: int32 [32], P('tm'), may hold values from 0 to 31, each once
- episode_id: int32 [32], replicated, may hold values from 0 to 3, never falling along the last dimension, each value on 1 to 16 neighbouring positions
- space_gain: float32 [2048], replicated, may hold values from 0.25 to 1.75
- space_qkv: bfloat16 [3, 2048, 2048], P(None, None, 'tensor'), as said below
- space_out: bfloat16 [2048, 2048], P('tensor'), may hold values from -0.125 to 0.125
- time_gain: float32 [2048], replicated, may hold values from 0.25 to 1.75
- time_qkv: bfloat16 [3, 2048, 2048], P(None, None, 'tensor'), as said below
- time_out: bfloat16 [2048, 2048], P('tensor'), may hold values from -0.125 to 0.125
Outputs:
- result: bfloat16 [32, 768, 2048], P('tm', None, 'tensor')
Inputs may be any that keep to these rules, and one draw needn't show every extreme that they name: pair_index names every encoder row exactly once. episode_id never falls along the frames; an episode has 1 to 16 frames. `space_qkv`: three stacked projection matrices, in the order query, key, value. `time_qkv`: three stacked projection matrices, in the order query, key, value.
All inputs are finite; a program needn't handle non-finite values.
Results may differ from a plain program's by a relative error of at most 0.012.
Values may be sent and summed in bfloat16 or wider, within the bound.
A program may use at most 64 MiB of HBM per device.

v0:
```python
import jax
import jax.numpy as jnp
from jax import lax
from jax.sharding import PartitionSpec as P

HEAD_DIM = 128


EPSILON = 1e-06


def fold_projection(weights, row_count, segment):
    flat_rows = segment.reshape(row_count, segment.shape[-1])
    return jnp.einsum("rc,icj->irj", flat_rows, weights, preferred_element_type=jnp.float32)


def space_frame(triple):
    query, keys, values = triple
    tokens_frame, columns = query.shape
    query = query.reshape(tokens_frame, columns // HEAD_DIM, HEAD_DIM)
    keys = keys.reshape(tokens_frame, columns // HEAD_DIM, HEAD_DIM)
    values = values.reshape(tokens_frame, columns // HEAD_DIM, HEAD_DIM)
    scores = jnp.einsum(
        "qhd,khd->hqk", query, keys, preferred_element_type=jnp.float32
    ) * HEAD_DIM ** (-0.5)
    probabilities = jax.nn.softmax(scores, -1).astype(jnp.bfloat16)
    mixture = jnp.einsum(
        "hqk,khd->qhd", probabilities, values, preferred_element_type=jnp.float32
    ).astype(jnp.bfloat16)
    return mixture.reshape(tokens_frame, columns)


def body(
    tokens,
    action_rows,
    pair_index,
    episode_id,
    space_gain,
    space_qkv,
    space_out,
    time_gain,
    time_qkv,
    time_out,
):
    frames_here, per_frame, share_width = tokens.shape
    width = share_width * lax.axis_size("tensor")
    columns = space_qkv.shape[2]
    row_count = frames_here * per_frame
    offset = lax.axis_index("tensor") * share_width
    every_row = lax.all_gather(action_rows, "tm", axis=0, tiled=True)
    frame_count = every_row.shape[0]
    picker = (pair_index[:, None] == jnp.arange(frame_count, dtype=jnp.int32)[None, :]).astype(
        jnp.bfloat16
    )
    action = jnp.dot(picker, every_row, preferred_element_type=jnp.float32)
    start = tokens.astype(jnp.float32) + action[:, None, :]
    squares = lax.psum(jnp.sum(start * start, -1), "tensor")
    factor = lax.rsqrt(squares / width + EPSILON)[..., None]
    space_normed = (
        start * factor * lax.dynamic_slice_in_dim(space_gain, offset, share_width)
    ).astype(jnp.bfloat16)
    space_proj = fold_projection(
        space_qkv, row_count, lax.all_gather(space_normed, "tensor", axis=2, tiled=True)
    ).astype(jnp.bfloat16)
    space_proj = space_proj.reshape(3, frames_here, per_frame, columns)
    attended = lax.map(space_frame, (space_proj[0], space_proj[1], space_proj[2]))
    partial_space = jnp.dot(
        attended.reshape(row_count, columns), space_out, preferred_element_type=jnp.float32
    ).reshape(frames_here, per_frame, width)
    middle = start + lax.psum_scatter(
        partial_space.astype(jnp.bfloat16), "tensor", scatter_dimension=2, tiled=True
    ).astype(jnp.float32)
    middle_squares = lax.psum(jnp.sum(middle * middle, -1), "tensor")
    middle_factor = lax.rsqrt(middle_squares / width + EPSILON)[..., None]
    time_normed = (
        middle * middle_factor * lax.dynamic_slice_in_dim(time_gain, offset, share_width)
    ).astype(jnp.bfloat16)
    time_proj = fold_projection(
        time_qkv, row_count, lax.all_gather(time_normed, "tensor", axis=2, tiled=True)
    ).astype(jnp.bfloat16)
    time_proj = time_proj.reshape(3, frames_here, per_frame, columns)
    moved = (
        lax.all_to_all(time_proj[0], "tm", split_axis=1, concat_axis=0, tiled=True),
        lax.all_to_all(time_proj[1], "tm", split_axis=1, concat_axis=0, tiled=True),
        lax.all_to_all(time_proj[2], "tm", split_axis=1, concat_axis=0, tiled=True),
    )
    query_time, keys_time, values_time = moved
    places = query_time.shape[1]
    heads_here = columns // HEAD_DIM
    query_time = query_time.reshape(frame_count, places, heads_here, HEAD_DIM)
    keys_time = keys_time.reshape(frame_count, places, heads_here, HEAD_DIM)
    values_time = values_time.reshape(frame_count, places, heads_here, HEAD_DIM)
    scores = jnp.einsum(
        "fphd,gphd->phfg", query_time, keys_time, preferred_element_type=jnp.float32
    ) * HEAD_DIM ** (-0.5)
    order = jnp.arange(frame_count, dtype=jnp.int32)
    allowed = (episode_id[:, None] == episode_id[None, :]) & (order[None, :] <= order[:, None])
    scores = jnp.where(allowed, scores, -1e30)
    probabilities = jax.nn.softmax(scores, -1).astype(jnp.bfloat16)
    mixture = jnp.einsum(
        "phfg,gphd->fphd", probabilities, values_time, preferred_element_type=jnp.float32
    ).astype(jnp.bfloat16)
    returned = lax.all_to_all(
        mixture.reshape(frame_count, places, columns), "tm", split_axis=0, concat_axis=1, tiled=True
    )
    partial_time = jnp.dot(
        returned.reshape(row_count, columns), time_out, preferred_element_type=jnp.float32
    ).reshape(frames_here, per_frame, width)
    return (
        middle
        + lax.psum_scatter(
            partial_time.astype(jnp.bfloat16), "tensor", scatter_dimension=2, tiled=True
        ).astype(jnp.float32)
    ).astype(jnp.bfloat16)


def solution(mesh):
    return jax.shard_map(
        body,
        mesh=mesh,
        in_specs=(
            P("tm", None, "tensor"),
            P("tm", "tensor"),
            P("tm"),
            P(),
            P(),
            P(None, None, "tensor"),
            P("tensor", None),
            P(),
            P(None, None, "tensor"),
            P("tensor", None),
        ),
        out_specs=P("tm", None, "tensor"),
        check_vma=False,
    )
```

profile of v0, /device:TPU:32, one launch (start us, length us, event | category | flops | bytes accessed | tf_op | source)
XLA Modules:
  0.0 409.3 jit_solution(3595024587277032656)
XLA Ops:
  6.5 24.8 %all-gather = bf16[32,1,256]{2,1,0:T(2,128)(2,1)S(1)} all-gather(bf16[1,1,256]{2,1,0:T(2,128)(2,1)} %bitcast.83), channel_id=1, replica_groups=mesh['tm'=32,'tensor'=8] {'tm'}, dimensions={0}, use_global_device_ids=true | all-gather | bytes 16896 | tf_op jit(solution)/shard_map/all_gather | solution.py:50
  32.1 1.2 multiply_reduce_fusion.2
  33.3 17.9 %psum.14 = f32[1,768]{1,0:T(1,128)S(1)} all-reduce(f32[1,768]{1,0:T(1,128)S(1)} %reduce_sum.42), channel_id=1, replica_groups=mesh['tm'=32,'tensor'=8] {'tensor'}, use_global_device_ids=true, to_apply=%region_1.0 | all-reduce | flops 768 | bytes 6144 | tf_op jit(solution)/shard_map/psum | solution.py:57
  52.0 1.9 multiply_convert_fusion.1
  54.0 53.1 %all-gather.4.cloned.1.call-done = bf16[1,768,2048]{2,1,0:T(8,128)(2,1)} async-done(((bf16[1,768,256]{2,1,0:T(8,128)(2,1)}), bf16[1,768,2048]{2,1,0:T(8,128)(2,1)}) %all-gather.4.cloned.1.call-update) | async-done | bytes 3145744 | tf_op jit(solution)/shard_map/all_gather | solution.py:63
  107.0 4.5 %fusion.23 = bf16[3,768,256]{1,2,0:T(8,128)(2,1)S(1)} fusion(bf16[3,2048,256]{2,1,0:T(8,128)(2,1)S(1)} %copy-done, bf16[1,768,2048]{2,1,0:T(8,128)(2,1)} %all-gather.4.cloned.1.call-done), kind=kOutput, calls=%fused_computation.20 | convolution fusion | flops 2416508928 | bytes 7471104 | tf_op jit(solution)/shard_map/rc,icj->irj/dot_general | solution.py:14
  111.6 1.0 fusion.47
  112.5 4.8 %fusion.48 = (f32[2,768]{1,0:T(2,128)S(1)}, f32[2,768,768]{1,2,0:T(8,128)}) fusion(bf16[768,2,128]{0,2,1:T(8,128)(2,1)} %bitcast.76, bf16[768,2,128]{0,2,1:T(8,128)(2,1)} %bitcast.75), kind=kOutput, calls=%fused_computation.55 | convolution fusion | flops 305529600 | bytes 5511168 | tf_op jit(solution)/shard_map/while/body/eval_jaxpr/sub | solution.py:26
  117.4 2.9 fusion.28
  120.3 2.7 fusion.9
  123.8 44.9 %reduce-scatter.3.cloned.1.call-done = bf16[1,768,256]{2,1,0:T(8,128)(2,1)} async-done(((bf16[1,768,2048]{2,1,0:T(8,128)(2,1)}), bf16[1,768,256]{2,1,0:T(8,128)(2,1)}) %reduce-scatter.3.cloned.1.call-update) | async-done | bytes 393232 | tf_op jit(solution)/shard_map/reduce_scatter | solution.py:70
  168.7 1.2 multiply_reduce_fusion.1
  169.9 15.6 %psum.15 = f32[1,768]{1,0:T(1,128)S(1)} all-reduce(f32[1,768]{1,0:T(1,128)S(1)} %reduce_sum.45), channel_id=1, replica_groups=mesh['tm'=32,'tensor'=8] {'tensor'}, use_global_device_ids=true, to_apply=%region_6.7 | all-reduce | flops 768 | bytes 6144 | tf_op jit(solution)/shard_map/psum | solution.py:73
  185.5 1.9 multiply_convert_fusion
  187.4 56.2 %all-gather.6.cloned.1.call-done = bf16[1,768,2048]{2,1,0:T(8,128)(2,1)} async-done(((bf16[1,768,256]{2,1,0:T(8,128)(2,1)}), bf16[1,768,2048]{2,1,0:T(8,128)(2,1)}) %all-gather.6.cloned.1.call-update) | async-done | bytes 3145744 | tf_op jit(solution)/shard_map/all_gather | solution.py:79
  243.6 5.4 %fusion.20 = bf16[3,768,256]{2,1,0:T(8,128)(2,1)S(1)} fusion(bf16[3,2048,256]{2,1,0:T(8,128)(2,1)} %param.18, bf16[1,768,2048]{2,1,0:T(8,128)(2,1)} %all-gather.6.cloned.1.call-done), kind=kOutput, calls=%fused_computation.19 | convolution fusion | flops 2416508928 | bytes 7471104 | tf_op jit(solution)/shard_map/rc,icj->irj/dot_general | solution.py:14
  249.0 1.0 fusion.46
  250.0 1.5 copy.70
  252.0 4.6 %reduce.12 = bf16[768,256]{1,0:T(8,128)(2,1)} reduce(bf16[768,1,256]{2,1,0:T(2,128)(2,1)} %bitcast.71, bf16[]{:T(256)} %broadcast.51), dimensions={1}, to_apply=%bitcast.69.reduce_sub_computation | reduce | bytes 786434
  256.6 1.8 reshape.134
  258.5 7.2 %all-to-all-start = ((bf16[32,2,3072]{2,1,0:T(2,128)(2,1)}), bf16[32,2,3072]{2,1,0:T(2,128)(2,1)}, u32[]{:S(2)}, u32[]{:S(2)}) async-start(bf16[32,2,3072]{2,1,0:T(2,128)(2,1)} %reshape.134), calls=%async_computation.1 | async-start | bytes 786432 | tf_op jit(solution)/shard_map/all_to_all | solution.py:85
  265.7 2.5 copy.68
  268.2 4.6 %reduce.13 = bf16[768,256]{1,0:T(8,128)(2,1)} reduce(bf16[768,1,256]{2,1,0:T(2,128)(2,1)} %bitcast.73, bf16[]{:T(256)} %broadcast.51), dimensions={1}, to_apply=%bitcast.67.reduce_sub_computation | reduce | bytes 786434
  272.8 1.9 reshape.136
  274.7 1.2 all-to-all-done
  275.9 6.2 %all-to-all-start.2 = ((bf16[32,2,3072]{2,1,0:T(2,128)(2,1)}), bf16[32,2,3072]{2,1,0:T(2,128)(2,1)}, u32[]{:S(2)}, u32[]{:S(2)}) async-start(bf16[32,2,3072]{2,1,0:T(2,128)(2,1)} %reshape.136), calls=%async_computation.3 | async-start | bytes 786432 | tf_op jit(solution)/shard_map/all_to_all | solution.py:84
  282.2 2.5 copy.69
  284.7 4.6 %reduce.14 = bf16[768,256]{1,0:T(8,128)(2,1)} reduce(bf16[768,1,256]{2,1,0:T(2,128)(2,1)} %bitcast.72, bf16[]{:T(256)} %broadcast.51), dimensions={1}, to_apply=%bitcast.68.reduce_sub_computation | reduce | bytes 786434
  289.3 1.8 reshape.138
  291.1 3.4 reshape.135
  294.6 7.4 %all-to-all-start.1 = ((bf16[32,2,3072]{2,1,0:T(2,128)(2,1)}), bf16[32,2,3072]{2,1,0:T(2,128)(2,1)}, u32[]{:S(2)}, u32[]{:S(2)}) async-start(bf16[32,2,3072]{2,1,0:T(2,128)(2,1)} %reshape.138), calls=%async_computation.2 | async-start | bytes 786432 | tf_op jit(solution)/shard_map/all_to_all | solution.py:83
  302.3 4.2 %bitcast_reduce_fusion.2 = bf16[768,256]{1,0:T(8,128)(2,1)} fusion(bf16[768,1,256]{2,1,0:T(2,128)(2,1)} %reshape.135), kind=kLoop, calls=%fused_computation.59 | loop fusion | bytes 786432 | tf_op jit(solution)/shard_map/all_to_all | solution.py:85
  306.5 1.8 reshape.118
  308.3 3.4 reshape.137
  311.7 4.2 %bitcast_reduce_fusion.1 = bf16[768,256]{1,0:T(8,128)(2,1)} fusion(bf16[768,1,256]{2,1,0:T(2,128)(2,1)} %reshape.137), kind=kLoop, calls=%fused_computation.58 | loop fusion | bytes 786432 | tf_op jit(solution)/shard_map/all_to_all | solution.py:84
  315.9 1.9 reshape.120
  317.8 3.4 reshape.139
  321.2 4.2 %bitcast_reduce_fusion = bf16[768,256]{1,0:T(8,128)(2,1)} fusion(bf16[768,1,256]{2,1,0:T(2,128)(2,1)} %reshape.139), kind=kLoop, calls=%fused_computation.57 | loop fusion | bytes 786432 | tf_op jit(solution)/shard_map/all_to_all | solution.py:83
  325.4 1.8 reshape.119
  327.2 1.4 fusion.27
  328.7 0.9 copy-done.4
  330.4 2.7 fusion.29
  333.1 2.0 copy.48
  335.1 2.0 reshape.121
  337.1 17.5 %all_to_all.16 = bf16[32,24,256]{2,1,0:T(8,128)(2,1)S(1)} all-to-all(bf16[32,24,256]{2,1,0:T(8,128)(2,1)} %reshape.121), channel_id=1, replica_groups=mesh['tm'=32,'tensor'=8] {'tm'}, dimensions={0} | all-to-all | bytes 786432 | tf_op jit(solution)/shard_map/all_to_all | solution.py:103
  354.6 3.9 fusion.10
  358.5 42.3 %reduce-scatter.5.cloned.1.call-done = bf16[1,768,256]{2,1,0:T(8,128)(2,1)} async-done(((bf16[1,768,2048]{2,1,0:T(8,128)(2,1)}), bf16[1,768,256]{2,1,0:T(8,128)(2,1)}) %reduce-scatter.5.cloned.1.call-update) | async-done | bytes 393232 | tf_op jit(solution)/shard_map/reduce_scatter | solution.py:111
  400.8 2.0 add_convert_fusion
  (29 shorter events, 3.6 us)
Async XLA Ops:
  6.5 100.5 %copy-start = (bf16[3,2048,256]{2,1,0:T(8,128)(2,1)S(1)}, bf16[3,2048,256]{2,1,0:T(8,128)(2,1)}, u32[]{:S(2)}) copy-start(bf16[3,2048,256]{2,1,0:T(8,128)(2,1)} %param.15) | copy-start | bytes 9437188
  6.5 100.5 %all-gather.4.cloned.1.call-start = ((), (), s32[]{:S(2)}) async-start(), calls=%async_computation.6 | async-start | bytes 3538944 | tf_op jit(solution)/shard_map/all_gather | solution.py:63
  53.9 114.8 %reduce-scatter.3.cloned.1.call-start = ((), (), s32[]{:S(2)}) async-start(), calls=%async_computation.7 | async-start | bytes 3538944 | tf_op jit(solution)/shard_map/reduce_scatter | solution.py:70
  117.4 2.9 copy-start.3
  120.3 48.4 %copy-start.1 = (bf16[1,768,256]{2,1,0:T(8,128)(2,1)S(1)}, bf16[1,768,256]{2,1,0:T(8,128)(2,1)}, u32[]{:S(2)}) copy-start(bf16[1,768,256]{2,1,0:T(8,128)(2,1)} %param.10) | copy-start | bytes 1179652
  123.0 120.6 %all-gather.6.cloned.1.call-start = ((), (), s32[]{:S(2)}) async-start(), calls=%async_computation.8 | async-start | bytes 3538944 | tf_op jit(solution)/shard_map/all_gather | solution.py:79
  252.0 30.1 %copy-start.2 = (s32[32]{0:T(128)S(1)}, s32[32]{0:T(128)}, u32[]{:S(2)}) copy-start(s32[32]{0:T(128)} %param.13) | copy-start | bytes 388
  258.5 17.4 %all-to-all-start = ((bf16[32,2,3072]{2,1,0:T(2,128)(2,1)}), bf16[32,2,3072]{2,1,0:T(2,128)(2,1)}, u32[]{:S(2)}, u32[]{:S(2)}) async-start(bf16[32,2,3072]{2,1,0:T(2,128)(2,1)} %reshape.134), calls=%async_computation.1 | async-start | bytes 786432 | tf_op jit(solution)/shard_map/all_to_all | solution.py:85
  275.9 18.7 %all-to-all-start.2 = ((bf16[32,2,3072]{2,1,0:T(2,128)(2,1)}), bf16[32,2,3072]{2,1,0:T(2,128)(2,1)}, u32[]{:S(2)}, u32[]{:S(2)}) async-start(bf16[32,2,3072]{2,1,0:T(2,128)(2,1)} %reshape.136), calls=%async_computation.3 | async-start | bytes 786432 | tf_op jit(solution)/shard_map/all_to_all | solution.py:84
  294.6 23.2 %all-to-all-start.1 = ((bf16[32,2,3072]{2,1,0:T(2,128)(2,1)}), bf16[32,2,3072]{2,1,0:T(2,128)(2,1)}, u32[]{:S(2)}, u32[]{:S(2)}) async-start(bf16[32,2,3072]{2,1,0:T(2,128)(2,1)} %reshape.138), calls=%async_computation.2 | async-start | bytes 786432 | tf_op jit(solution)/shard_map/all_to_all | solution.py:83
  302.0 98.7 %reduce-scatter.5.cloned.1.call-start = ((), (), s32[]{:S(2)}) async-start(), calls=%async_computation.9 | async-start | bytes 3538944 | tf_op jit(solution)/shard_map/reduce_scatter | solution.py:111
  328.7 0.9 copy-start.4
Sparse Core Ops, SparseCore 0:
  54.0 52.9 all-gather.3
  123.1 45.5 reduce-scatter.2
  187.6 55.9 all-gather.5
  358.6 42.0 reduce-scatter.4
where the time goes:
time: 412 us; the launch traced here: 409 us
  waiting for transfers between devices  198 us (48%)
  blocking collectives  75.7 us (18%)
  local copies, waits for them, and re-layouts  49.3 us (12%)
  matrix products  28.5 us (7%)
  other arithmetic  23.1 us (6%)
  starting transfers between devices  21.2 us (5%)
  between operations  13.9 us (3%)
    all_gather x1, waiting for transfers between devices, body(): lax.all_gather(time_normed, 'tensor', axis=2, tiled=True)  56.2 us
    all_gather x1, waiting for transfers between devices, body(): lax.all_gather(space_normed, 'tensor', axis=2, tiled=True)  53.1 us
    reduce_scatter x1, waiting for transfers between devices, body(): lax.psum_scatter(partial_space.astype(jnp.bfloat16), 'tensor', scatter_di...  44.9 us
    reduce_scatter x1, waiting for transfers between devices, body(): lax.psum_scatter(partial_time.astype(jnp.bfloat16), 'tensor', scatter_dim...  42.3 us
    all_gather x1, blocking collectives, body(): every_row = lax.all_gather(action_rows, 'tm', axis=0, tiled=True)  24.8 us
    psum x1, blocking collectives, body(): squares = lax.psum(jnp.sum(start * start, -1), 'tensor')  17.9 us
    all_to_all x1, blocking collectives, body(): lax.all_to_all(mixture.reshape(frame_count, places, columns), 'tm', split...  17.5 us
    unnamed x17, local copies, waits for them, and re-layouts  17.2 us
  transfers between devices with their start and end apart: 7, of which 5 were waited for; matrix products, arithmetic and copies ran while one was open for 9% of the time, Pallas kernels for 0%

commit v1 on v0

v1 whole, which is shorter than its diff:
```python
import jax
import jax.numpy as jnp
from jax import lax
from jax.experimental import pallas as pl
from jax.experimental.pallas import tpu as pltpu
from jax.sharding import PartitionSpec as P

MESH = pl.DeviceIdType.MESH
HEAD_DIM = 128
EPSILON = 1e-06
SCALE = HEAD_DIM ** (-0.5)
TM, Z = 32, 8
CHUNKS, ROWS, COLS, WIDTH = 3, 256, 256, 2048
TOKENS = CHUNKS * ROWS
PLACES = ROWS // TM
BF, F32 = jnp.bfloat16, jnp.float32


def kernel(
    tokens, action, pair, episode, space_gain, space_qkv, space_out, time_gain, time_qkv, time_out,
    out,
    tokf, af, tfb, wq, wt, wo, to, arow, act, actz, row, xn, mid, midz, qkv, mask, snd, rcv, snd2, rcv2,
    ag_send, ag_recv, w_send, w_recv, loc, one_send, one_recv, a2a_send, a2a_recv,
):
    tm, z = lax.axis_index("tm"), lax.axis_index("tensor")
    y, x, k = tm // 8, lax.rem(tm // 2, 4), lax.rem(tm, 2)
    chip = tm // 2
    zr, zl = lax.rem(z + 1, Z), lax.rem(z + Z - 1, Z)

    def remote(src, dst, ssem, rsem, t, zz):
        return pltpu.make_async_remote_copy(
            src_ref=src, dst_ref=dst, send_sem=ssem, recv_sem=rsem, device_id=(t, zz), device_id_type=MESH
        )

    def bulk(ref, sem):
        pltpu.make_async_copy(ref, ref, sem).wait()

    def each(n, me, fn):
        def step(j, carry):
            fn(lax.rem(me + j, n))
            return carry
        lax.fori_loop(1, n, step, 0)

    own = pl.multiple_of(z * COLS, COLS)

    load_wq = pltpu.make_async_copy(space_qkv, wq, loc.at[0])
    load_wt = pltpu.make_async_copy(time_qkv, wt, loc.at[1])
    load_wq.start()
    load_wt.start()
    load_tok = pltpu.make_async_copy(tokens.at[0], tokf.at[:, pl.ds(own, COLS)], loc.at[2])
    load_tok.start()
    arow[...] = jnp.broadcast_to(action[...].astype(F32), (8, COLS)).astype(BF)

    barrier = pltpu.get_barrier_semaphore()
    each(TM, tm, lambda t: pl.semaphore_signal(barrier, inc=1, device_id=(t, z), device_id_type=MESH))
    each(Z, z, lambda q: pl.semaphore_signal(barrier, inc=1, device_id=(tm, q), device_id_type=MESH))
    pl.semaphore_wait(barrier, TM - 1 + Z - 1)

    def gather(n, view, half, first):
        def copy(d, s, i):
            origin = lax.rem(z + (Z - s if d == 0 else s), Z)
            if s == 3:
                src = dst = half(i, origin, d)
            else:
                dst = view(i, origin)
                src = first(i) if s == 0 else dst
            return remote(src, dst, ag_send.at[n, d, s, i], ag_recv.at[n, d, s, i], tm, zr if d == 0 else zl)

        def send(s, i):
            for d in (0, 1):
                if s:
                    copy(d, s - 1, i).wait_recv()
                copy(d, s, i).start()

        def finish(i):
            for d in (0, 1):
                copy(d, 3, i).wait_recv()

        def drain():
            for d in (0, 1):
                for s in range(4):
                    for i in range(CHUNKS):
                        copy(d, s, i).wait_send()

        return send, finish, drain

    def flat(buf):
        def view(i, origin):
            return buf.at[pl.ds(ROWS * i, ROWS), pl.ds(pl.multiple_of(origin * COLS, COLS), COLS)]

        def half(i, origin, d):
            return buf.at[
                pl.ds(ROWS * i + d * (ROWS // 2), ROWS // 2), pl.ds(pl.multiple_of(origin * COLS, COLS), COLS)
            ]
        return view, half

    tok_view, tok_half = flat(tokf)
    tok_send, tok_finish, tok_drain = gather(
        0, tok_view, tok_half, lambda i: tokens.at[0, pl.ds(ROWS * i, ROWS), :]
    )
    a_view, a_half = flat(af)
    a_send, a_finish, a_drain = gather(1, a_view, a_half, lambda i: a_view(i, z))
    t_send, t_finish, t_drain = gather(
        2,
        lambda i, origin: tfb.at[origin, i],
        lambda i, origin, d: tfb.at[origin, i, pl.ds(d * (TM // 2), TM // 2)],
        lambda i: rcv2.at[i],
    )

    p, r = y + k * (x - y), x + k * (y - x)

    def place(pp, rr):
        return ((pp * 4 + rr) * (1 - k) + (rr * 4 + pp) * k) * 2 + k

    p1, p3, p2 = lax.rem(p + 1, 4), lax.rem(p + 3, 4), lax.rem(p + 2, 4)
    r1, r3 = lax.rem(r + 1, 4), lax.rem(r + 3, 4)
    w_src = space_out.at[pl.ds(pl.multiple_of(k * 128, 128), 128), pl.ds(pl.multiple_of(chip * 128, 128), 128)]

    def w0(q):
        return remote(w_src, wo.at[k, p, r, z], one_send.at[0], one_recv.at[0], tm, q)

    def w0_local():
        return pltpu.make_async_copy(w_src, wo.at[k, p, r, z], one_recv.at[0])

    def w1(d):
        return remote(wo.at[k, p, r], wo.at[k, p, r], w_send.at[d], w_recv.at[d], place(p, r1 if d == 0 else r3), z)

    def w1b(d):
        ref = wo.at[k, p, r3 if d == 0 else r1, pl.ds(4 * d, 4)]
        return remote(ref, ref, w_send.at[2 + d], w_recv.at[2 + d], place(p, r1 if d == 0 else r3), z)

    def w2(d):
        return remote(wo.at[k, p], wo.at[k, p], w_send.at[4 + d], w_recv.at[4 + d], place(p1 if d == 0 else p3, r), z)

    def w2b(d):
        ref = wo.at[k, p3 if d == 0 else p1, pl.ds(2 * d, 2)]
        return remote(ref, ref, w_send.at[6 + d], w_recv.at[6 + d], place(p1 if d == 0 else p3, r), z)

    def w3(n):
        ref = wo.at[k, (p, p1, p3, p2)[n]]
        return remote(ref, ref, w_send.at[8 + n], w_recv.at[8 + n], tm + 1 - 2 * k, z)

    def t_src(q):
        return time_out.at[
            pl.ds(pl.multiple_of(chip * 16, 16), 16), pl.ds(pl.multiple_of(q * COLS, COLS), COLS)
        ]

    def t0(q):
        return remote(t_src(q), to.at[z, chip], one_send.at[1], one_recv.at[1], tm, q)

    def t0_local():
        return pltpu.make_async_copy(t_src(z), to.at[z, chip], one_recv.at[1])

    def t1(c):
        return remote(to.at[:, chip], to.at[:, chip], one_send.at[2], one_recv.at[2], c * 2 + k, z)

    def act_copy(t):
        return remote(arow, act.at[tm], one_send.at[3], one_recv.at[3], t, z)

    def actz_copy(q):
        return remote(actz.at[z], actz.at[z], one_send.at[4], one_recv.at[4], tm, q)

    each(Z, z, lambda q: w0(q).start())
    w0_local().start()
    each(TM, tm, lambda t: act_copy(t).start())
    act_local = pltpu.make_async_copy(arow, act.at[tm], one_recv.at[3])
    act_local.start()
    for i in range(CHUNKS):
        tok_send(0, i)

    one = lax.broadcasted_iota(jnp.int32, (ROWS, 128), 0)
    two = lax.broadcasted_iota(jnp.int32, (8, ROWS), 1)
    one_f, two_f = lax.shift_right_logical(one, 3), lax.shift_right_logical(two, 3)
    one_e, two_e = jnp.zeros_like(one), jnp.zeros_like(two)
    for f in range(TM):
        one_e = jnp.where(one_f == f, episode[f], one_e)
        two_e = jnp.where(two_f == f, episode[f], two_e)

    def wide_row(v):
        return jnp.concatenate([v, v], axis=1)

    def wide_col(v):
        return jnp.broadcast_to(v[0:1], (ROWS, ROWS))

    allowed = (
        (wide_row(one_e) == wide_col(two_e))
        & (wide_col(two_f) <= wide_row(one_f))
        & (wide_row(one & 7) == wide_col(two & 7))
    )
    mask[...] = jnp.where(allowed, 1.0, 0.0)

    bulk(act, one_recv.at[3])
    actz[z] = act[pair[0]]
    each(Z, z, lambda q: actz_copy(q).start())

    for i in range(CHUNKS):
        tok_send(1, i)
    bulk(wo.at[k, p, r], one_recv.at[0])
    w1(0).start()
    w1(1).start()
    tok_send(2, 0)
    tok_send(2, 1)
    for d in (0, 1):
        w1(d).wait_recv()
        w1b(d).start()
    tok_send(2, 2)
    for d in (0, 1):
        w1b(d).wait_recv()
    w2(0).start()
    w2(1).start()
    w3(0).start()
    load_wq.wait()
    load_tok.wait()
    bulk(actz.at[pl.ds(0, Z - 1)], one_recv.at[4])
    for q in range(Z):
        row[:, COLS * q : COLS * (q + 1)] = actz[q].astype(F32)
    for i in range(CHUNKS):
        tok_send(3, i)
    each(Z, z, lambda q: t0(q).start())
    t0_local().start()

    STEP = 32

    def normed(get, gain):
        def tile(n, carry):
            at = pl.multiple_of(n * STEP, STEP)
            v = get(at)
            factor = lax.rsqrt(jnp.sum(v * v, -1, keepdims=True) * (1.0 / WIDTH) + EPSILON)
            xn[pl.ds(at, STEP), :] = (v * factor * gain[...]).astype(BF)
            return carry
        lax.fori_loop(0, ROWS // STEP, tile, 0)

    for i in range(CHUNKS):
        tok_finish(i)

        def start_tile(at, i=i):
            return tokf[pl.ds(ROWS * i + at, STEP), :].astype(F32) + row[0:1, :]

        normed(start_tile, space_gain)
        for n in range(3):
            qkv[n, ROWS * i : ROWS * (i + 1), :] = jnp.dot(xn[...], wq[n], preferred_element_type=F32).astype(BF)
        if i == 0:
            for d in (0, 1):
                w2(d).wait_recv()
                w2b(d).start()
            w3(1).start()
            w3(2).start()
            bulk(to.at[:, 0], one_recv.at[1])
            each(TM // 2, chip, lambda c: t1(c).start())

    def attend(i):
        for h in range(2):
            cols = slice(HEAD_DIM * h, HEAD_DIM * (h + 1))
            s = lax.dot_general(
                qkv[0, ROWS * i : ROWS * (i + 1), cols], qkv[1, :, cols], (((1,), (1,)), ((), ())),
                preferred_element_type=F32,
            ) * SCALE
            e = jnp.exp(s - jnp.max(s, -1, keepdims=True))
            prob = (e / jnp.sum(e, -1, keepdims=True)).astype(BF)
            o = jnp.dot(prob, qkv[2, :, cols], preferred_element_type=F32)
            at = pl.multiple_of(z * COLS + HEAD_DIM * h, HEAD_DIM)
            af[ROWS * i : ROWS * (i + 1), pl.ds(at, HEAD_DIM)] = o.astype(BF)

    def project(i, lo, hi):
        rows = slice(ROWS * i, ROWS * (i + 1))

        def tile(j, carry):
            yy, xx = j // 2, 2 * lax.rem(j, 2)

            def rhs(kk):
                a, b = ((yy, xx), (yy, xx + 1)) if kk == 0 else ((xx, yy), (xx + 1, yy))
                return jnp.concatenate(
                    [wo[kk, a[0], a[1]].reshape(1024, 128), wo[kk, b[0], b[1]].reshape(1024, 128)], axis=1
                )

            def lhs(kk):
                return jnp.concatenate(
                    [af[rows, COLS * q + 128 * kk : COLS * q + 128 * (kk + 1)] for q in range(Z)], axis=1
                )

            at = pl.multiple_of(j * COLS, COLS)
            total = jnp.dot(lhs(0), rhs(0), preferred_element_type=F32)
            total = total + jnp.dot(lhs(1), rhs(1), preferred_element_type=F32)
            start = tokf[rows, pl.ds(at, COLS)].astype(F32) + row[0:1, pl.ds(at, COLS)]
            mid[:, pl.ds(at, COLS)] = start + total
            return carry
        lax.fori_loop(lo, hi, tile, 0)

    def renorm(i):
        normed(lambda at: mid[pl.ds(at, STEP), :], time_gain)
        midz[ROWS * i : ROWS * (i + 1), :] = mid[:, pl.ds(own, COLS)]

    def qkv_copy(i, t):
        return remote(snd.at[i, t], rcv.at[i, tm], a2a_send.at[0, i], a2a_recv.at[0, i], t, z)

    def scatter(i):
        for n in range(3):
            v = jnp.dot(xn[...], wt[n], preferred_element_type=F32)
            snd[i, :, :, COLS * n : COLS * (n + 1)] = v.reshape(TM, PLACES, COLS).astype(BF)
        each(TM, tm, lambda t: qkv_copy(i, t).start())
        pltpu.make_async_copy(snd.at[i, tm], rcv.at[i, tm], a2a_recv.at[0, i]).start()

    def mix_copy(i, t):
        return remote(snd2.at[i, t], rcv2.at[i, tm], a2a_send.at[1, i], a2a_recv.at[1, i], t, z)

    def mix(i):
        bulk(rcv.at[i], a2a_recv.at[0, i])

        def take(n, h):
            at = COLS * n + HEAD_DIM * h
            return rcv[i, :, :, at : at + HEAD_DIM].astype(F32).reshape(ROWS, HEAD_DIM).astype(BF)

        for h in range(2):
            s = lax.dot_general(
                take(0, h), take(1, h), (((1,), (1,)), ((), ())), preferred_element_type=F32
            ) * SCALE
            s = jnp.where(mask[...] > 0.5, s, -1e30)
            e = jnp.exp(s - jnp.max(s, -1, keepdims=True))
            prob = (e / jnp.sum(e, -1, keepdims=True)).astype(BF)
            o = jnp.dot(prob, take(2, h), preferred_element_type=F32)
            snd2[i, :, :, HEAD_DIM * h : HEAD_DIM * (h + 1)] = o.reshape(TM, PLACES, HEAD_DIM).astype(BF)
        each(TM, tm, lambda t: mix_copy(i, t).start())
        pltpu.make_async_copy(snd2.at[i, tm], rcv2.at[i, tm], a2a_recv.at[1, i]).start()

    def back(i):
        bulk(rcv2.at[i], a2a_recv.at[1, i])
        t_send(0, i)
        pltpu.make_async_copy(rcv2.at[i], tfb.at[z, i], loc.at[3 + i]).start()

    def finish(i):
        t_finish(i)
        pltpu.make_async_copy(rcv2.at[i], tfb.at[z, i], loc.at[3 + i]).wait()
        lhs = jnp.concatenate([tfb[q, i].astype(F32).reshape(ROWS, COLS).astype(BF) for q in range(Z)], axis=1)
        update = jnp.dot(lhs, to[...].reshape(WIDTH, COLS), preferred_element_type=F32)
        rows = slice(ROWS * i, ROWS * (i + 1))
        out[0, rows, :] = (midz[rows, :] + update).astype(BF)

    attend(0)
    a_send(0, 0)
    attend(1)
    a_send(0, 1)
    a_send(1, 0)
    for d in (0, 1):
        w2b(d).wait_recv()
    w3(3).start()
    attend(2)
    a_send(0, 2)
    a_send(2, 0)
    a_send(1, 1)
    a_send(3, 0)
    a_send(1, 2)
    a_send(2, 1)
    load_wt.wait()
    for n in range(4):
        w3(n).wait_recv()
    a_finish(0)
    project(0, 0, 4)
    project(0, 4, 8)
    a_send(2, 2)
    a_send(3, 1)
    renorm(0)
    scatter(0)
    a_send(3, 2)
    a_finish(1)
    project(1, 0, 8)
    mix(0)
    renorm(1)
    scatter(1)
    back(0)
    a_finish(2)
    project(2, 0, 4)
    mix(1)
    project(2, 4, 8)
    t_send(1, 0)
    renorm(2)
    back(1)
    scatter(2)
    t_send(2, 0)
    t_send(1, 1)
    t_send(3, 0)
    mix(2)
    t_send(2, 1)
    back(2)
    t_send(3, 1)
    bulk(to.at[:, pl.ds(0, TM // 2 - 1)], one_recv.at[2])
    finish(0)
    t_send(1, 2)
    t_send(2, 2)
    finish(1)
    t_send(3, 2)
    finish(2)

    tok_drain()
    a_drain()
    t_drain()
    bulk(wo.at[0, 0, 0, pl.ds(0, Z - 1)], one_send.at[0])
    bulk(to.at[pl.ds(0, Z - 1), 0], one_send.at[1])
    bulk(to.at[:, pl.ds(0, TM // 2 - 1)], one_send.at[2])
    bulk(act.at[pl.ds(0, TM - 1)], one_send.at[3])
    bulk(actz.at[pl.ds(0, Z - 1)], one_send.at[4])
    for d in (0, 1):
        w1(d).wait_send()
        w1b(d).wait_send()
        w2(d).wait_send()
        w2b(d).wait_send()
    for n in range(4):
        w3(n).wait_send()
    for i in range(CHUNKS):
        bulk(snd.at[i, pl.ds(0, TM - 1)], a2a_send.at[0, i])
        bulk(snd2.at[i, pl.ds(0, TM - 1)], a2a_send.at[1, i])


def body(
    tokens, action_rows, pair_index, episode_id, space_gain, space_qkv, space_out, time_gain, time_qkv, time_out
):
    any_, vmem, smem = (pl.BlockSpec(memory_space=m) for m in (pl.ANY, pltpu.VMEM, pltpu.SMEM))
    dma = pltpu.SemaphoreType.DMA
    return pl.pallas_call(
        kernel,
        out_shape=jax.ShapeDtypeStruct(tokens.shape, BF),
        in_specs=[any_, vmem, smem, smem, vmem, any_, any_, vmem, any_, any_],
        out_specs=vmem,
        scratch_shapes=[
            pltpu.VMEM((TOKENS, WIDTH), BF),
            pltpu.VMEM((TOKENS, WIDTH), BF),
            pltpu.VMEM((Z, CHUNKS, TM, PLACES, COLS), BF),
            pltpu.VMEM((3, WIDTH, COLS), BF),
            pltpu.VMEM((3, WIDTH, COLS), BF),
            pltpu.VMEM((2, 4, 4, Z, 128, 128), BF),
            pltpu.VMEM((Z, TM // 2, 16, COLS), BF),
            pltpu.VMEM((8, COLS), BF),
            pltpu.VMEM((TM, 8, COLS), BF),
            pltpu.VMEM((Z, 8, COLS), BF),
            pltpu.VMEM((8, WIDTH), F32),
            pltpu.VMEM((ROWS, WIDTH), BF),
            pltpu.VMEM((ROWS, WIDTH), F32),
            pltpu.VMEM((TOKENS, COLS), F32),
            pltpu.VMEM((3, TOKENS, COLS), BF),
            pltpu.VMEM((ROWS, ROWS), F32),
            pltpu.VMEM((CHUNKS, TM, PLACES, 3 * COLS), BF),
            pltpu.VMEM((CHUNKS, TM, PLACES, 3 * COLS), BF),
            pltpu.VMEM((CHUNKS, TM, PLACES, COLS), BF),
            pltpu.VMEM((CHUNKS, TM, PLACES, COLS), BF),
            dma((3, 2, 4, CHUNKS)),
            dma((3, 2, 4, CHUNKS)),
            dma((12,)),
            dma((12,)),
            dma((6,)),
            dma((5,)),
            dma((5,)),
            dma((2, CHUNKS)),
            dma((2, CHUNKS)),
        ],
        compiler_params=pltpu.CompilerParams(
            collective_id=0, has_side_effects=True, vmem_limit_bytes=60 * 1024 * 1024
        ),
    )(
        tokens, action_rows, pair_index, episode_id, space_gain.reshape(1, WIDTH), space_qkv, space_out,
        time_gain.reshape(1, WIDTH), time_qkv, time_out,
    )


def solution(mesh):
    return jax.shard_map(
        body,
        mesh=mesh,
        in_specs=(
            P("tm", None, "tensor"),
            P("tm", "tensor"),
            P("tm"),
            P(),
            P(),
            P(None, None, "tensor"),
            P("tensor", None),
            P(),
            P(None, None, "tensor"),
            P("tensor", None),
        ),
        out_specs=P("tm", None, "tensor"),
        check_vma=False,
    )
```

time: 412 us -> 151 us (0.37)
  waiting for transfers between devices: 198 us -> 0 us
  Pallas kernels: 0 us -> 148 us
  blocking collectives: 75.7 us -> 0 us
  local copies, waits for them, and re-layouts: 49.3 us -> 1.77 us
  matrix products: 28.5 us -> 0 us
  other arithmetic: 23.1 us -> 0 us
  starting transfers between devices: 21.2 us -> 0 us
  between operations: 13.9 us -> 0.66 us
    pallas_call x0 -> x1, Pallas kernels: none -> 148 us  [body(): pl.pallas_call(kernel, out_shape=jax.ShapeDtypeStruct(tokens.shape, BF),...]
    all_gather x2 -> x0, waiting for transfers between devices: 109 us -> none  [the longest x1 56.2 us: body(): lax.all_gather(time_normed, 'tensor', axis=2, tiled=True)]
    reduce_scatter x2 -> x0, waiting for transfers between devices: 87.1 us -> none  [the longest x1 44.9 us: body(): lax.psum_scatter(partial_space.astype(jnp.bfloat16), 'tensor', scatter_di...]
    psum x2 -> x0, blocking collectives: 33.4 us -> none  [the longest x1 17.9 us: body(): squares = lax.psum(jnp.sum(start * start, -1), 'tensor')]
    all_gather x1 -> x0, blocking collectives: 24.8 us -> none  [body(): every_row = lax.all_gather(action_rows, 'tm', axis=0, tiled=True)]
    dot_general x8 -> x0, matrix products: 23.7 us -> none  [the longest x2 9.98 us: fold_projection(): jnp.einsum('rc,icj->irj', flat_rows, weights, preferred_element_type=jnp....]
    all_to_all x3 -> x0, starting transfers between devices: 20.9 us -> none  [the longest x1 7.43 us: body(): lax.all_to_all(time_proj[0], 'tm', split_axis=1, concat_axis=0, tiled=True)]
    all_to_all x1 -> x0, blocking collectives: 17.5 us -> none  [body(): lax.all_to_all(mixture.reshape(frame_count, places, columns), 'tm', split...]
  transfers between devices with their start and end apart: 7 -> 0, of which waited for: 5 -> 0; matrix products, arithmetic and copies ran while one was open for 9% -> 0% of each run, Pallas kernels for 0% -> 0%
where the time goes in v1:
time: 151 us; the launch traced here: 150 us
  Pallas kernels  148 us (98%)
  local copies, waits for them, and re-layouts  1.77 us (1%)
    pallas_call x1, Pallas kernels, body(): pl.pallas_call(kernel, out_shape=jax.ShapeDtypeStruct(tokens.shape, BF),...  148 us

profile of v1, /device:TPU:32, one launch (start us, length us, event | category | flops | bytes accessed | tf_op | source)
XLA Modules:
  0.0 150.3 jit_solution(9914354283430638970)
XLA Ops:
  0.7 147.9 %shard_map.100 = bf16[1,768,256]{2,1,0:T(8,128)(2,1)} custom-call(bf16[1,768,256]{2,1,0:T(8,128)(2,1)} %tokens.1, bf16[1,256]{1,0:T(2,128)(2,1)} %action.1, s32[1]{0:T(128)S(6)} %copy.12.pair, s32[32]{0:T(128)} %episode.1, f32[1,2048]{1,0:T(1,128)} %bitcast.2, bf16[3,2048,256]{2,1,0:T(8,128)(2,1)} %space_qkv.1, bf16[256,2048]{1,0:T(8,128)(2,1)} %space_out.1, ...), custom_call_target="tpu_custom_call" | custom-call | tf_op jit(solution)/shard_map/pallas_call | solution.py:418
  148.6 1.8 %copy.13 = bf16[1,768,256]{2,1,0:T(8,128)(2,1)} copy(bf16[1,768,256]{2,1,0:T(8,128)(2,1)} %shard_map.100) | data formatting | bytes 786432

commit v2 on v1

--- a/solution.py
+++ b/solution.py
@@ -14,13 +14,32 @@
 TOKENS = CHUNKS * ROWS
 PLACES = ROWS // TM
 BF, F32 = jnp.bfloat16, jnp.float32
+ORDER = [
+    ("w0", 0), ("act",), ("t0",), ("w0", 1), ("k", 0, 0, 0), ("mask",), ("k", 0, 0, 1), ("k", 0, 1, 0),
+    ("k", 0, 1, 1), ("w0", 2), ("sel",), ("t1",), ("k", 1, 0, 0), ("k", 1, 0, 1), ("k", 1, 1, 0), ("k", 1, 1, 1),
+    ("w0", 3), ("k", 2, 0, 0), ("k", 2, 0, 1), ("k", 2, 1, 0), ("k", 2, 1, 1), ("w1",), ("wp", 0), ("k", 0, 2, 0),
+    ("k", 3, 0, 0), ("k", 3, 0, 1), ("k", 0, 2, 1), ("k", 3, 1, 0), ("k", 3, 1, 1), ("w1b",), ("wp", 1), ("wp", 2),
+    ("k", 1, 2, 0), ("q", 0), ("k", 1, 2, 1), ("wpb", 0), ("q", 1), ("wp", 3), ("k", 2, 2, 0), ("k", 2, 2, 1),
+    ("k", 3, 2, 0), ("wpb", 1), ("k", 3, 2, 1), ("q", 2), ("wpb", 2), ("att", 0), ("a", 0, 0, 0), ("a", 0, 0, 1),
+    ("w3", 0), ("att", 1), ("a", 0, 1, 0), ("att", 2), ("a", 0, 1, 1), ("a", 1, 0, 0), ("wpb", 3), ("a", 1, 0, 1),
+    ("w3", 1), ("a", 1, 1, 0), ("a", 1, 1, 1), ("w3", 2), ("a", 2, 0, 0), ("w3", 3), ("a", 2, 0, 1), ("a", 2, 1, 0),
+    ("a", 2, 1, 1), ("a", 3, 0, 0), ("a", 3, 0, 1), ("a", 0, 2, 0), ("a", 3, 1, 0), ("a", 3, 1, 1), ("a", 0, 2, 1),
+    ("p", 0, 0), ("p", 0, 1), ("a", 1, 2, 0), ("p", 0, 2), ("p", 0, 3), ("r", 0), ("a", 1, 2, 1), ("s", 0),
+    ("a", 2, 2, 0), ("p", 1, 0), ("p", 1, 1), ("a", 2, 2, 1), ("p", 1, 2), ("p", 1, 3), ("a", 3, 2, 0), ("r", 1),
+    ("a", 3, 2, 1), ("s", 1), ("p", 2, 0), ("p", 2, 1), ("m", 0), ("p", 2, 2), ("p", 2, 3), ("r", 2), ("s", 2),
+    ("m", 1), ("t", 0, 0, 0), ("t", 0, 0, 1), ("t", 1, 0, 0), ("t", 1, 0, 1), ("t", 2, 0, 0), ("m", 2),
+    ("t", 2, 0, 1), ("t", 0, 1, 0), ("t", 3, 0, 0), ("t", 0, 1, 1), ("t", 3, 0, 1), ("t", 1, 1, 0), ("t", 0, 2, 0),
+    ("t", 1, 1, 1), ("f", 0), ("t", 0, 2, 1), ("t", 2, 1, 0), ("t", 1, 2, 0), ("t", 2, 1, 1), ("t", 1, 2, 1),
+    ("t", 3, 1, 0), ("t", 2, 2, 0), ("t", 3, 1, 1), ("t", 2, 2, 1), ("t", 3, 2, 0), ("f", 1), ("t", 3, 2, 1),
+    ("f", 2),
+]
 
 
 def kernel(
     tokens, action, pair, episode, space_gain, space_qkv, space_out, time_gain, time_qkv, time_out,
     out,
     tokf, af, tfb, wq, wt, wo, to, arow, act, actz, row, xn, mid, midz, qkv, mask, snd, rcv, snd2, rcv2,
-    ag_send, ag_recv, w_send, w_recv, loc, one_send, one_recv, a2a_send, a2a_recv,
+    tok_ss, tok_rs, a_ss, a_rs, t_ss, t_rs, w0_ss, w0_rs, w_send, w_recv, loc, one_send, one_recv, a2a_send, a2a_recv,
 ):
     tm, z = lax.axis_index("tm"), lax.axis_index("tensor")
     y, x, k = tm // 8, lax.rem(tm // 2, 4), lax.rem(tm, 2)
@@ -56,55 +75,65 @@
     each(Z, z, lambda q: pl.semaphore_signal(barrier, inc=1, device_id=(tm, q), device_id_type=MESH))
     pl.semaphore_wait(barrier, TM - 1 + Z - 1)
 
-    def gather(n, view, half, first):
-        def copy(d, s, i):
+    seen = set()
+
+    def once(key, wait):
+        if key not in seen:
+            seen.add(key)
+            wait()
+
+    def gather(name, view, first, ssem, rsem, chunks):
+        def copy(d, s, i, h):
             origin = lax.rem(z + (Z - s if d == 0 else s), Z)
-            if s == 3:
-                src = dst = half(i, origin, d)
-            else:
-                dst = view(i, origin)
-                src = first(i) if s == 0 else dst
-            return remote(src, dst, ag_send.at[n, d, s, i], ag_recv.at[n, d, s, i], tm, zr if d == 0 else zl)
-
-        def send(s, i):
+            dst = view(i, h, origin)
+            src = first(i, h) if s == 0 else dst
+            return remote(src, dst, ssem.at[d, s, i, h], rsem.at[d, s, i, h], tm, zr if d == 0 else zl)
+
+        def arrived(d, s, i, h):
+            once((name, d, s, i, h), lambda: copy(d, s, i, h).wait_recv())
+
+        def send(s, i, h):
             for d in (0, 1):
-                if s:
-                    copy(d, s - 1, i).wait_recv()
-                copy(d, s, i).start()
+                if s < 3 or h == d:
+                    if s:
+                        arrived(d, s - 1, i, h)
+                    copy(d, s, i, h).start()
 
         def finish(i):
             for d in (0, 1):
-                copy(d, 3, i).wait_recv()
+                for s in range(4):
+                    for h in (0, 1):
+                        if s < 3 or h == d:
+                            arrived(d, s, i, h)
 
         def drain():
-            for d in (0, 1):
-                for s in range(4):
-                    for i in range(CHUNKS):
-                        copy(d, s, i).wait_send()
+            for i in range(chunks):
+                for d in (0, 1):
+                    for s in range(4):
+                        for h in (0, 1):
+                            if s < 3 or h == d:
+                                copy(d, s, i, h).wait_send()
 
         return send, finish, drain
 
+    HALF = ROWS // 2
+
     def flat(buf):
-        def view(i, origin):
-            return buf.at[pl.ds(ROWS * i, ROWS), pl.ds(pl.multiple_of(origin * COLS, COLS), COLS)]
-
-        def half(i, origin, d):
+        def view(i, h, origin):
             return buf.at[
-                pl.ds(ROWS * i + d * (ROWS // 2), ROWS // 2), pl.ds(pl.multiple_of(origin * COLS, COLS), COLS)
+                pl.ds(ROWS * i + HALF * h, HALF), pl.ds(pl.multiple_of(origin * COLS, COLS), COLS)
             ]
-        return view, half
-
-    tok_view, tok_half = flat(tokf)
+        return view
+
     tok_send, tok_finish, tok_drain = gather(
-        0, tok_view, tok_half, lambda i: tokens.at[0, pl.ds(ROWS * i, ROWS), :]
+        0, flat(tokf), lambda i, h: tokens.at[0, pl.ds(ROWS * i + HALF * h, HALF), :], tok_ss, tok_rs, CHUNKS
     )
-    a_view, a_half = flat(af)
-    a_send, a_finish, a_drain = gather(1, a_view, a_half, lambda i: a_view(i, z))
+    a_view = flat(af)
+    a_send, a_finish, a_drain = gather(1, a_view, lambda i, h: a_view(i, h, z), a_ss, a_rs, CHUNKS)
     t_send, t_finish, t_drain = gather(
-        2,
-        lambda i, origin: tfb.at[origin, i],
-        lambda i, origin, d: tfb.at[origin, i, pl.ds(d * (TM // 2), TM // 2)],
-        lambda i: rcv2.at[i],
+        2, lambda i, h, origin: tfb.at[origin, i, pl.ds(h * (TM // 2), TM // 2)],
+        lambda i, h: rcv2.at[i, pl.ds(h * (TM // 2), TM // 2)],
+        t_ss, t_rs, CHUNKS,
     )
 
     p, r = y + k * (x - y), x + k * (y - x)
@@ -112,15 +141,18 @@
     def place(pp, rr):
         return ((pp * 4 + rr) * (1 - k) + (rr * 4 + pp) * k) * 2 + k
 
-    p1, p3, p2 = lax.rem(p + 1, 4), lax.rem(p + 3, 4), lax.rem(p + 2, 4)
-    r1, r3 = lax.rem(r + 1, 4), lax.rem(r + 3, 4)
+    p1, p3 = lax.rem(p + 1, 4), lax.rem(p + 3, 4)
+    r1, r3, r2 = lax.rem(r + 1, 4), lax.rem(r + 3, 4), lax.rem(r + 2, 4)
     w_src = space_out.at[pl.ds(pl.multiple_of(k * 128, 128), 128), pl.ds(pl.multiple_of(chip * 128, 128), 128)]
 
-    def w0(q):
-        return remote(w_src, wo.at[k, p, r, z], one_send.at[0], one_recv.at[0], tm, q)
-
-    def w0_local():
-        return pltpu.make_async_copy(w_src, wo.at[k, p, r, z], one_recv.at[0])
+    w0_send, w0_finish, w0_drain = gather(
+        3, lambda i, h, origin: wo.at[k, p, r, origin, pl.ds(64 * h, 64)],
+        lambda i, h: space_out.at[
+            pl.ds(pl.multiple_of(k * 128 + 64 * h, 64), 64), pl.ds(pl.multiple_of(chip * 128, 128), 128)
+        ],
+        w0_ss, w0_rs, 1,
+    )
+    w0_local = pltpu.make_async_copy(w_src, wo.at[k, p, r, z], loc.at[6])
 
     def w1(d):
         return remote(wo.at[k, p, r], wo.at[k, p, r], w_send.at[d], w_recv.at[d], place(p, r1 if d == 0 else r3), z)
@@ -129,16 +161,22 @@
         ref = wo.at[k, p, r3 if d == 0 else r1, pl.ds(4 * d, 4)]
         return remote(ref, ref, w_send.at[2 + d], w_recv.at[2 + d], place(p, r1 if d == 0 else r3), z)
 
-    def w2(d):
-        return remote(wo.at[k, p], wo.at[k, p], w_send.at[4 + d], w_recv.at[4 + d], place(p1 if d == 0 else p3, r), z)
-
-    def w2b(d):
-        ref = wo.at[k, p3 if d == 0 else p1, pl.ds(2 * d, 2)]
-        return remote(ref, ref, w_send.at[6 + d], w_recv.at[6 + d], place(p1 if d == 0 else p3, r), z)
-
-    def w3(n):
-        ref = wo.at[k, (p, p1, p3, p2)[n]]
-        return remote(ref, ref, w_send.at[8 + n], w_recv.at[8 + n], tm + 1 - 2 * k, z)
+    def wp(e, d):
+        ref = wo.at[k, p, (r, r3, r1, r2)[e]]
+        n = 4 + 2 * e + d
+        return remote(ref, ref, w_send.at[n], w_recv.at[n], place(p1 if d == 0 else p3, r), z)
+
+    def wpb(e, d):
+        ref = wo.at[k, p3 if d == 0 else p1, (r, r3, r1, r2)[e], pl.ds(4 * d, 4)]
+        n = 12 + 2 * e + d
+        return remote(ref, ref, w_send.at[n], w_recv.at[n], place(p1 if d == 0 else p3, r), z)
+
+    def w3(e):
+        ref = wo.at[k, :, (r, r3, r1, r2)[e]]
+        return remote(ref, ref, w_send.at[20 + e], w_recv.at[20 + e], tm + 1 - 2 * k, z)
+
+    def w_arrived(name, fn, *at):
+        once((name, at), lambda: fn(*at).wait_recv())
 
     def t_src(q):
         return time_out.at[
@@ -160,64 +198,27 @@
     def actz_copy(q):
         return remote(actz.at[z], actz.at[z], one_send.at[4], one_recv.at[4], tm, q)
 
-    each(Z, z, lambda q: w0(q).start())
-    w0_local().start()
-    each(TM, tm, lambda t: act_copy(t).start())
-    act_local = pltpu.make_async_copy(arow, act.at[tm], one_recv.at[3])
-    act_local.start()
-    for i in range(CHUNKS):
-        tok_send(0, i)
-
-    one = lax.broadcasted_iota(jnp.int32, (ROWS, 128), 0)
-    two = lax.broadcasted_iota(jnp.int32, (8, ROWS), 1)
-    one_f, two_f = lax.shift_right_logical(one, 3), lax.shift_right_logical(two, 3)
-    one_e, two_e = jnp.zeros_like(one), jnp.zeros_like(two)
-    for f in range(TM):
-        one_e = jnp.where(one_f == f, episode[f], one_e)
-        two_e = jnp.where(two_f == f, episode[f], two_e)
-
-    def wide_row(v):
-        return jnp.concatenate([v, v], axis=1)
-
-    def wide_col(v):
-        return jnp.broadcast_to(v[0:1], (ROWS, ROWS))
-
-    allowed = (
-        (wide_row(one_e) == wide_col(two_e))
-        & (wide_col(two_f) <= wide_row(one_f))
-        & (wide_row(one & 7) == wide_col(two & 7))
-    )
-    mask[...] = jnp.where(allowed, 1.0, 0.0)
-
-    bulk(act, one_recv.at[3])
-    actz[z] = act[pair[0]]
-    each(Z, z, lambda q: actz_copy(q).start())
-
-    for i in range(CHUNKS):
-        tok_send(1, i)
-    bulk(wo.at[k, p, r], one_recv.at[0])
-    w1(0).start()
-    w1(1).start()
-    tok_send(2, 0)
-    tok_send(2, 1)
-    for d in (0, 1):
-        w1(d).wait_recv()
-        w1b(d).start()
-    tok_send(2, 2)
-    for d in (0, 1):
-        w1b(d).wait_recv()
-    w2(0).start()
-    w2(1).start()
-    w3(0).start()
-    load_wq.wait()
-    load_tok.wait()
-    bulk(actz.at[pl.ds(0, Z - 1)], one_recv.at[4])
-    for q in range(Z):
-        row[:, COLS * q : COLS * (q + 1)] = actz[q].astype(F32)
-    for i in range(CHUNKS):
-        tok_send(3, i)
-    each(Z, z, lambda q: t0(q).start())
-    t0_local().start()
+    def build_mask():
+        one = lax.broadcasted_iota(jnp.int32, (ROWS, 128), 0)
+        two = lax.broadcasted_iota(jnp.int32, (8, ROWS), 1)
+        one_f, two_f = lax.shift_right_logical(one, 3), lax.shift_right_logical(two, 3)
+        one_e, two_e = jnp.zeros_like(one), jnp.zeros_like(two)
+        for f in range(TM):
+            one_e = jnp.where(one_f == f, episode[f], one_e)
+            two_e = jnp.where(two_f == f, episode[f], two_e)
+
+        def wide_row(v):
+            return jnp.concatenate([v, v], axis=1)
+
+        def wide_col(v):
+            return jnp.broadcast_to(v[0:1], (ROWS, ROWS))
+
+        allowed = (
+            (wide_row(one_e) == wide_col(two_e))
+            & (wide_col(two_f) <= wide_row(one_f))
+            & (wide_row(one & 7) == wide_col(two & 7))
+        )
+        mask[...] = jnp.where(allowed, 1.0, 0.0)
 
     STEP = 32
 
@@ -230,23 +231,21 @@
             return carry
         lax.fori_loop(0, ROWS // STEP, tile, 0)
 
-    for i in range(CHUNKS):
+    def spatial(i):
+        if i == 0:
+            load_wq.wait()
+            load_tok.wait()
+            bulk(actz.at[pl.ds(0, Z - 1)], one_recv.at[4])
+            for q in range(Z):
+                row[:, COLS * q : COLS * (q + 1)] = actz[q].astype(F32)
         tok_finish(i)
 
-        def start_tile(at, i=i):
+        def start_tile(at):
             return tokf[pl.ds(ROWS * i + at, STEP), :].astype(F32) + row[0:1, :]
 
         normed(start_tile, space_gain)
         for n in range(3):
             qkv[n, ROWS * i : ROWS * (i + 1), :] = jnp.dot(xn[...], wq[n], preferred_element_type=F32).astype(BF)
-        if i == 0:
-            for d in (0, 1):
-                w2(d).wait_recv()
-                w2b(d).start()
-            w3(1).start()
-            w3(2).start()
-            bulk(to.at[:, 0], one_recv.at[1])
-            each(TM // 2, chip, lambda c: t1(c).start())
 
     def attend(i):
         for h in range(2):
@@ -324,7 +323,6 @@
 
     def back(i):
         bulk(rcv2.at[i], a2a_recv.at[1, i])
-        t_send(0, i)
         pltpu.make_async_copy(rcv2.at[i], tfb.at[z, i], loc.at[3 + i]).start()
 
     def finish(i):
@@ -335,65 +333,93 @@
         rows = slice(ROWS * i, ROWS * (i + 1))
         out[0, rows, :] = (midz[rows, :] + update).astype(BF)
 
-    attend(0)
-    a_send(0, 0)
-    attend(1)
-    a_send(0, 1)
-    a_send(1, 0)
-    for d in (0, 1):
-        w2b(d).wait_recv()
-    w3(3).start()
-    attend(2)
-    a_send(0, 2)
-    a_send(2, 0)
-    a_send(1, 1)
-    a_send(3, 0)
-    a_send(1, 2)
-    a_send(2, 1)
-    load_wt.wait()
-    for n in range(4):
-        w3(n).wait_recv()
-    a_finish(0)
-    project(0, 0, 4)
-    project(0, 4, 8)
-    a_send(2, 2)
-    a_send(3, 1)
-    renorm(0)
-    scatter(0)
-    a_send(3, 2)
-    a_finish(1)
-    project(1, 0, 8)
-    mix(0)
-    renorm(1)
-    scatter(1)
-    back(0)
-    a_finish(2)
-    project(2, 0, 4)
-    mix(1)
-    project(2, 4, 8)
-    t_send(1, 0)
-    renorm(2)
-    back(1)
-    scatter(2)
-    t_send(2, 0)
-    t_send(1, 1)
-    t_send(3, 0)
-    mix(2)
-    t_send(2, 1)
-    back(2)
-    t_send(3, 1)
-    bulk(to.at[:, pl.ds(0, TM // 2 - 1)], one_recv.at[2])
-    finish(0)
-    t_send(1, 2)
-    t_send(2, 2)
-    finish(1)
-    t_send(3, 2)
-    finish(2)
+    def act_spread():
+        each(TM, tm, lambda t: act_copy(t).start())
+        pltpu.make_async_copy(arow, act.at[tm], one_recv.at[3]).start()
+
+    def act_choose():
+        bulk(act, one_recv.at[3])
+        actz[z] = act[pair[0]]
+        each(Z, z, lambda q: actz_copy(q).start())
+
+    def w0_step(s):
+        if s == 0:
+            w0_local.start()
+        for h in (0, 1):
+            w0_send(s, 0, h)
+
+    def w1_step():
+        w0_finish(0)
+        w0_local.wait()
+        w1(0).start()
+        w1(1).start()
+
+    def w1b_step():
+        for d in (0, 1):
+            w_arrived("w1", w1, d)
+            w1b(d).start()
+
+    def wp_step(e):
+        if e in (1, 2):
+            w_arrived("w1", w1, e - 1)
+        if e == 3:
+            w_arrived("w1b", w1b, 0)
+            w_arrived("w1b", w1b, 1)
+        wp(e, 0).start()
+        wp(e, 1).start()
+
+    def wpb_step(e):
+        for d in (0, 1):
+            w_arrived("wp", wp, e, d)
+            wpb(e, d).start()
+
+    def w3_step(e):
+        for d in (0, 1):
+            w_arrived("wpb", wpb, e, d)
+        w3(e).start()
+
+    def t0_step():
+        each(Z, z, lambda q: t0(q).start())
+        t0_local().start()
+
+    def t1_step():
+        bulk(to.at[:, 0], one_recv.at[1])
+        each(TM // 2, chip, lambda c: t1(c).start())
+
+    def p_step(i, j):
+        if j == 0:
+            for e in range(4):
+                w_arrived("w3", w3, e)
+            a_finish(i)
+        project(i, 2 * j, 2 * j + 2)
+
+    def s_step(i):
+        if i == 0:
+            load_wt.wait()
+        scatter(i)
+
+    def t_step(s, i, h):
+        if s == 0:
+            once(("back", i), lambda: back(i))
+        t_send(s, i, h)
+
+    def f_step(i):
+        if i == 0:
+            bulk(to.at[:, pl.ds(0, TM // 2 - 1)], one_recv.at[2])
+        finish(i)
+
+    run = {
+        "k": tok_send, "a": a_send, "t": t_step, "w0": w0_step, "w1": w1_step, "w1b": w1b_step, "wp": wp_step,
+        "wpb": wpb_step, "w3": w3_step, "act": act_spread, "sel": act_choose, "mask": build_mask, "t0": t0_step,
+        "t1": t1_step, "q": spatial, "att": attend, "p": p_step, "r": renorm, "s": s_step, "m": mix, "f": f_step,
+    }
+    for name, *at in ORDER:
+        run[name](*at)
 
     tok_drain()
     a_drain()
     t_drain()
-    bulk(wo.at[0, 0, 0, pl.ds(0, Z - 1)], one_send.at[0])
+    w0_drain()
     bulk(to.at[pl.ds(0, Z - 1), 0], one_send.at[1])
     bulk(to.at[:, pl.ds(0, TM // 2 - 1)], one_send.at[2])
     bulk(act.at[pl.ds(0, TM - 1)], one_send.at[3])
@@ -401,10 +427,11 @@
     for d in (0, 1):
         w1(d).wait_send()
         w1b(d).wait_send()
-        w2(d).wait_send()
-        w2b(d).wait_send()
-    for n in range(4):
-        w3(n).wait_send()
+        for e in range(4):
+            wp(e, d).wait_send()
+            wpb(e, d).wait_send()
+    for e in range(4):
+        w3(e).wait_send()
     for i in range(CHUNKS):
         bulk(snd.at[i, pl.ds(0, TM - 1)], a2a_send.at[0, i])
         bulk(snd2.at[i, pl.ds(0, TM - 1)], a2a_send.at[1, i])
@@ -413,12 +440,12 @@
 def body(
     tokens, action_rows, pair_index, episode_id, space_gain, space_qkv, space_out, time_gain, time_qkv, time_out
 ):
-    any_, vmem, smem = (pl.BlockSpec(memory_space=m) for m in (pl.ANY, pltpu.VMEM, pltpu.SMEM))
+    hbm, vmem, smem = (pl.BlockSpec(memory_space=m) for m in (pltpu.HBM, pltpu.VMEM, pltpu.SMEM))
     dma = pltpu.SemaphoreType.DMA
     return pl.pallas_call(
         kernel,
         out_shape=jax.ShapeDtypeStruct(tokens.shape, BF),
-        in_specs=[any_, vmem, smem, smem, vmem, any_, any_, vmem, any_, any_],
+        in_specs=[hbm, vmem, smem, smem, vmem, hbm, hbm, vmem, hbm, hbm],
         out_specs=vmem,
         scratch_shapes=[
             pltpu.VMEM((TOKENS, WIDTH), BF),
@@ -441,11 +468,17 @@
             pltpu.VMEM((CHUNKS, TM, PLACES, 3 * COLS), BF),
             pltpu.VMEM((CHUNKS, TM, PLACES, COLS), BF),
             pltpu.VMEM((CHUNKS, TM, PLACES, COLS), BF),
-            dma((3, 2, 4, CHUNKS)),
-            dma((3, 2, 4, CHUNKS)),
-            dma((12,)),
-            dma((12,)),
-            dma((6,)),
+            dma((2, 4, CHUNKS, 2)),
+            dma((2, 4, CHUNKS, 2)),
+            dma((2, 4, CHUNKS, 2)),
+            dma((2, 4, CHUNKS, 2)),
+            dma((2, 4, CHUNKS, 2)),
+            dma((2, 4, CHUNKS, 2)),
+            dma((2, 4, 1, 2)),
+            dma((2, 4, 1, 2)),
+            dma((24,)),
+            dma((24,)),
+            dma((7,)),
             dma((5,)),
             dma((5,)),
             dma((2, CHUNKS)),

time: 151 us -> 146 us (0.967)
  Pallas kernels: 148 us -> 144 us
    pallas_call x1, Pallas kernels: 148 us -> 144 us  [body(): pl.pallas_call(kernel, out_shape=jax.ShapeDtypeStruct(tokens.shape, BF),...]
where the time goes in v2:
time: 146 us
  Pallas kernels  144 us (99%)
  local copies, waits for them, and re-layouts  1.77 us (1%)
    pallas_call x1, Pallas kernels, body(): pl.pallas_call(kernel, out_shape=jax.ShapeDtypeStruct(tokens.shape, BF),...  144 us

profile of v2, /device:TPU:32, one launch (start us, length us, event | category | flops | bytes accessed | tf_op | source)
XLA Modules:
  0.0 145.9 jit_solution(17654251739902347194)
XLA Ops:
  0.7 143.5 %shard_map.100 = bf16[1,768,256]{2,1,0:T(8,128)(2,1)} custom-call(bf16[1,768,256]{2,1,0:T(8,128)(2,1)} %tokens.1, bf16[1,256]{1,0:T(2,128)(2,1)} %action.1, s32[1]{0:T(128)S(6)} %copy.12.pair, s32[32]{0:T(128)} %episode.1, f32[1,2048]{1,0:T(1,128)} %bitcast.2, bf16[3,2048,256]{2,1,0:T(8,128)(2,1)} %space_qkv.1, bf16[256,2048]{1,0:T(8,128)(2,1)} %space_out.1, ...), custom_call_target="tpu_custom_call" | custom-call | tf_op jit(solution)/shard_map/pallas_call | solution.py:445
  144.2 1.8 %copy.13 = bf16[1,768,256]{2,1,0:T(8,128)(2,1)} copy(bf16[1,768,256]{2,1,0:T(8,128)(2,1)} %shard_map.100) | data formatting | bytes 786432

commit v3 on v2

--- a/solution.py
+++ b/solution.py
@@ -39,7 +39,7 @@
     tokens, action, pair, episode, space_gain, space_qkv, space_out, time_gain, time_qkv, time_out,
     out,
     tokf, af, tfb, wq, wt, wo, to, arow, act, actz, row, xn, mid, midz, qkv, mask, snd, rcv, snd2, rcv2,
-    tok_ss, tok_rs, a_ss, a_rs, t_ss, t_rs, w0_ss, w0_rs, w_send, w_recv, loc, one_send, one_recv, a2a_send, a2a_recv,
+    ring_ss, tok_rs, a_rs, t_rs, w0_rs, w_send, w_recv, loc, one_send, one_recv, a2a_send, a2a_recv,
 ):
     tm, z = lax.axis_index("tm"), lax.axis_index("tensor")
     y, x, k = tm // 8, lax.rem(tm // 2, 4), lax.rem(tm, 2)
@@ -56,9 +56,9 @@
 
     def each(n, me, fn):
         def step(j, carry):
-            fn(lax.rem(me + j, n))
+            fn(lax.rem(me + 1 + lax.rem(j + 9, n - 1), n))
             return carry
-        lax.fori_loop(1, n, step, 0)
+        lax.fori_loop(1, n, step, 0, unroll=True)
 
     own = pl.multiple_of(z * COLS, COLS)
 
@@ -87,7 +87,7 @@
             origin = lax.rem(z + (Z - s if d == 0 else s), Z)
             dst = view(i, h, origin)
             src = first(i, h) if s == 0 else dst
-            return remote(src, dst, ssem.at[d, s, i, h], rsem.at[d, s, i, h], tm, zr if d == 0 else zl)
+            return remote(src, dst, ssem, rsem.at[d, s, i, h], tm, zr if d == 0 else zl)
 
         def arrived(d, s, i, h):
             once((name, d, s, i, h), lambda: copy(d, s, i, h).wait_recv())
@@ -106,15 +106,7 @@
                         if s < 3 or h == d:
                             arrived(d, s, i, h)
 
-        def drain():
-            for i in range(chunks):
-                for d in (0, 1):
-                    for s in range(4):
-                        for h in (0, 1):
-                            if s < 3 or h == d:
-                                copy(d, s, i, h).wait_send()
-
-        return send, finish, drain
+        return send, finish
 
     HALF = ROWS // 2
 
@@ -125,15 +117,15 @@
             ]
         return view
 
-    tok_send, tok_finish, tok_drain = gather(
-        0, flat(tokf), lambda i, h: tokens.at[0, pl.ds(ROWS * i + HALF * h, HALF), :], tok_ss, tok_rs, CHUNKS
+    tok_send, tok_finish = gather(
+        0, flat(tokf), lambda i, h: tokens.at[0, pl.ds(ROWS * i + HALF * h, HALF), :], ring_ss.at[0], tok_rs, CHUNKS
     )
     a_view = flat(af)
-    a_send, a_finish, a_drain = gather(1, a_view, lambda i, h: a_view(i, h, z), a_ss, a_rs, CHUNKS)
-    t_send, t_finish, t_drain = gather(
+    a_send, a_finish = gather(1, a_view, lambda i, h: a_view(i, h, z), ring_ss.at[1], a_rs, CHUNKS)
+    t_send, t_finish = gather(
         2, lambda i, h, origin: tfb.at[origin, i, pl.ds(h * (TM // 2), TM // 2)],
         lambda i, h: rcv2.at[i, pl.ds(h * (TM // 2), TM // 2)],
-        t_ss, t_rs, CHUNKS,
+        ring_ss.at[2], t_rs, CHUNKS,
     )
 
     p, r = y + k * (x - y), x + k * (y - x)
@@ -145,35 +137,35 @@
     r1, r3, r2 = lax.rem(r + 1, 4), lax.rem(r + 3, 4), lax.rem(r + 2, 4)
     w_src = space_out.at[pl.ds(pl.multiple_of(k * 128, 128), 128), pl.ds(pl.multiple_of(chip * 128, 128), 128)]
 
-    w0_send, w0_finish, w0_drain = gather(
+    w0_send, w0_finish = gather(
         3, lambda i, h, origin: wo.at[k, p, r, origin, pl.ds(64 * h, 64)],
         lambda i, h: space_out.at[
             pl.ds(pl.multiple_of(k * 128 + 64 * h, 64), 64), pl.ds(pl.multiple_of(chip * 128, 128), 128)
         ],
-        w0_ss, w0_rs, 1,
+        ring_ss.at[3], w0_rs, 1,
     )
     w0_local = pltpu.make_async_copy(w_src, wo.at[k, p, r, z], loc.at[6])
 
     def w1(d):
-        return remote(wo.at[k, p, r], wo.at[k, p, r], w_send.at[d], w_recv.at[d], place(p, r1 if d == 0 else r3), z)
+        return remote(wo.at[k, p, r], wo.at[k, p, r], w_send.at[0], w_recv.at[d], place(p, r1 if d == 0 else r3), z)
 
     def w1b(d):
         ref = wo.at[k, p, r3 if d == 0 else r1, pl.ds(4 * d, 4)]
-        return remote(ref, ref, w_send.at[2 + d], w_recv.at[2 + d], place(p, r1 if d == 0 else r3), z)
+        return remote(ref, ref, w_send.at[0], w_recv.at[2 + d], place(p, r1 if d == 0 else r3), z)
 
     def wp(e, d):
         ref = wo.at[k, p, (r, r3, r1, r2)[e]]
         n = 4 + 2 * e + d
-        return remote(ref, ref, w_send.at[n], w_recv.at[n], place(p1 if d == 0 else p3, r), z)
+        return remote(ref, ref, w_send.at[1], w_recv.at[n], place(p1 if d == 0 else p3, r), z)
 
     def wpb(e, d):
         ref = wo.at[k, p3 if d == 0 else p1, (r, r3, r1, r2)[e], pl.ds(4 * d, 4)]
         n = 12 + 2 * e + d
-        return remote(ref, ref, w_send.at[n], w_recv.at[n], place(p1 if d == 0 else p3, r), z)
+        return remote(ref, ref, w_send.at[1], w_recv.at[n], place(p1 if d == 0 else p3, r), z)
 
     def w3(e):
         ref = wo.at[k, :, (r, r3, r1, r2)[e]]
-        return remote(ref, ref, w_send.at[20 + e], w_recv.at[20 + e], tm + 1 - 2 * k, z)
+        return remote(ref, ref, w_send.at[2], w_recv.at[20 + e], tm + 1 - 2 * k, z)
 
     def w_arrived(name, fn, *at):
         once((name, at), lambda: fn(*at).wait_recv())
@@ -416,22 +408,18 @@
     for name, *at in ORDER:
         run[name](*at)
 
-    tok_drain()
-    a_drain()
-    t_drain()
-    w0_drain()
+    sent = WIDTH - COLS
+    bulk(tokf.at[:, pl.ds(0, sent)], ring_ss.at[0])
+    bulk(af.at[:, pl.ds(0, sent)], ring_ss.at[1])
+    bulk(tfb.at[pl.ds(0, Z - 1)], ring_ss.at[2])
+    bulk(wo.at[0, 0, 0, pl.ds(0, Z - 1)], ring_ss.at[3])
     bulk(to.at[pl.ds(0, Z - 1), 0], one_send.at[1])
     bulk(to.at[:, pl.ds(0, TM // 2 - 1)], one_send.at[2])
     bulk(act.at[pl.ds(0, TM - 1)], one_send.at[3])
     bulk(actz.at[pl.ds(0, Z - 1)], one_send.at[4])
-    for d in (0, 1):
-        w1(d).wait_send()
-        w1b(d).wait_send()
-        for e in range(4):
-            wp(e, d).wait_send()
-            wpb(e, d).wait_send()
-    for e in range(4):
-        w3(e).wait_send()
+    bulk(wo.at[0, 0, pl.ds(0, 3)], w_send.at[0])
+    bulk(wo.at[0, pl.ds(0, 3)], w_send.at[1])
+    bulk(wo.at[0], w_send.at[2])
     for i in range(CHUNKS):
         bulk(snd.at[i, pl.ds(0, TM - 1)], a2a_send.at[0, i])
         bulk(snd2.at[i, pl.ds(0, TM - 1)], a2a_send.at[1, i])
@@ -468,15 +456,12 @@
             pltpu.VMEM((CHUNKS, TM, PLACES, 3 * COLS), BF),
             pltpu.VMEM((CHUNKS, TM, PLACES, COLS), BF),
             pltpu.VMEM((CHUNKS, TM, PLACES, COLS), BF),
-            dma((2, 4, CHUNKS, 2)),
-            dma((2, 4, CHUNKS, 2)),
-            dma((2, 4, CHUNKS, 2)),
+            dma((4,)),
             dma((2, 4, CHUNKS, 2)),
             dma((2, 4, CHUNKS, 2)),
             dma((2, 4, CHUNKS, 2)),
             dma((2, 4, 1, 2)),
-            dma((2, 4, 1, 2)),
-            dma((24,)),
+            dma((3,)),
             dma((24,)),
             dma((7,)),
             dma((5,)),

time: 146 us -> 144 us (0.986)
  Pallas kernels: 144 us -> 141 us
    pallas_call x1, Pallas kernels: 144 us -> 141 us  [body(): pl.pallas_call(kernel, out_shape=jax.ShapeDtypeStruct(tokens.shape, BF),...]
where the time goes in v3:
time: 144 us; the launch traced here: 143 us
  Pallas kernels  141 us (98%)
  local copies, waits for them, and re-layouts  1.77 us (1%)
    pallas_call x1, Pallas kernels, body(): pl.pallas_call(kernel, out_shape=jax.ShapeDtypeStruct(tokens.shape, BF),...  141 us

profile of v3, /device:TPU:32, one launch (start us, length us, event | category | flops | bytes accessed | tf_op | source)
XLA Modules:
  0.0 143.4 jit_solution(16249008562215354137)
XLA Ops:
  0.7 141.0 %shard_map.100 = bf16[1,768,256]{2,1,0:T(8,128)(2,1)} custom-call(bf16[1,768,256]{2,1,0:T(8,128)(2,1)} %tokens.1, bf16[1,256]{1,0:T(2,128)(2,1)} %action.1, s32[1]{0:T(128)S(6)} %copy.12.pair, s32[32]{0:T(128)} %episode.1, f32[1,2048]{1,0:T(1,128)} %bitcast.2, bf16[3,2048,256]{2,1,0:T(8,128)(2,1)} %space_qkv.1, bf16[256,2048]{1,0:T(8,128)(2,1)} %space_out.1, ...), custom_call_target="tpu_custom_call" | custom-call | tf_op jit(solution)/shard_map/pallas_call | solution.py:433
  141.6 1.8 %copy.13 = bf16[1,768,256]{2,1,0:T(8,128)(2,1)} copy(bf16[1,768,256]{2,1,0:T(8,128)(2,1)} %shard_map.100) | data formatting | bytes 786432
